TPU v7x, 256 devices: a whole 4x4x8 slice. The times are simulated.
256 devices in a mesh: seq: 64 (over x, z, core), head: 4 (over y).
Axes of the slice: x: 4, y: 4, z: 8, core: 2. Of those that a mesh axis runs over, the one named last changes fastest.
Arguments:
- queries: bfloat16 [16384, 64, 128], P(('seq', 'head')), may hold values from -64 to 64
- key_vectors: bfloat16 [16384, 64, 128], P(('seq', 'head')), may hold values from -5 to 5
- value_vectors: bfloat16 [16384, 64, 128], P(('seq', 'head')), may hold values from -6 to 6
- key_blocks: int32 [128, 12], P('seq'), may hold values from -1 to 125, as said below
Outputs:
- attended: bfloat16 [16384, 64, 128], P(('seq', 'head'))
Inputs may be any that keep to these rules, and one draw needn't show every extreme that they name: `key_blocks`: entries 2j and 2j+1 of row b are -1 or distinct blocks c with c // 2 == b // 2 - 2**j, never b - 1.
All inputs are finite; a program needn't handle non-finite values.
Results may differ from a plain program's by a relative error of at most 0.004.
Values may be sent and summed in bfloat16 or wider, within the bound.
A program may use at most 192 MiB of HBM per device.

v0:
```python
import math
import jax
import jax.numpy as jnp
from jax import lax
from jax.sharding import PartitionSpec as P

BLOCK = 128
LEVELS = 6


def from_behind(value, axis, by):
    size = lax.axis_size(axis)
    pairs = [(i, i + by) for i in range(size) if 0 <= i + by < size]
    return lax.ppermute(value, axis, pairs)


def absorb(carried, scores, apply_values):
    running_max, running_sum, weighted = carried
    new_max = jnp.maximum(running_max, jnp.max(scores, axis=-1))
    factor = jnp.exp(running_max - new_max)
    weights = jnp.exp(scores - new_max[..., None])
    running_sum = running_sum * factor + jnp.sum(weights, axis=-1)
    weighted = weighted * jnp.transpose(factor, (0, 2, 1))[..., None] + apply_values(
        weights.astype(jnp.bfloat16)
    )
    return (new_max, running_sum, weighted)


def local(queries, key_vectors, value_vectors, key_blocks):
    query_local, key_local, value_local = (
        lax.all_to_all(queries, "head", split_axis=1, concat_axis=0, tiled=True),
        lax.all_to_all(key_vectors, "head", split_axis=1, concat_axis=0, tiled=True),
        lax.all_to_all(value_vectors, "head", split_axis=1, concat_axis=0, tiled=True),
    )
    local_rows, head_count, head_width = query_local.shape
    blocks = local_rows // BLOCK
    device = lax.axis_index("seq")
    inverse_root = 1.0 / math.sqrt(head_width)
    query_tiles = query_local.reshape(blocks, BLOCK, head_count, head_width)
    query_ids = device * blocks + jnp.arange(blocks, dtype=jnp.int32)
    causal = jnp.arange(BLOCK)[:, None] >= jnp.arange(BLOCK)[None, :]
    carried = (
        jnp.full((blocks, head_count, BLOCK), -1e30, jnp.float32),
        jnp.zeros((blocks, head_count, BLOCK), jnp.float32),
        jnp.zeros((blocks, BLOCK, head_count, head_width), jnp.float32),
    )

    def dense_set(carried, near_keys, near_values, key_ids, with_diagonal):
        key_count = key_ids.shape[0]
        scores = (
            jnp.einsum("bqhd,nhd->bhqn", query_tiles, near_keys, preferred_element_type=jnp.float32)
            * inverse_root
        )
        scores = scores.reshape(blocks, head_count, BLOCK, key_count, BLOCK)
        listed = jnp.any(key_blocks[:, :, None] == key_ids[None, None, :], axis=1)
        window = key_ids[None, :] == query_ids[:, None] - 1
        allowed = (listed | window) & (key_ids >= 0)[None, :]
        allowed = allowed[:, None, None, :, None]
        if with_diagonal:
            diagonal = key_ids[None, :] == query_ids[:, None]
            allowed = allowed | diagonal[:, None, None, :, None] & causal[None, None, :, None, :]
        scores = jnp.where(allowed, scores, jnp.float32(-1e30)).reshape(
            blocks, head_count, BLOCK, key_count * BLOCK
        )

        def apply_values(rounded):
            return jnp.einsum(
                "bhqn,nhd->bqhd", rounded, near_values, preferred_element_type=jnp.float32
            )

        return absorb(carried, scores, apply_values)

    carried = dense_set(carried, key_local, value_local, query_ids, True)
    far_keys = key_local
    far_values = value_local
    for section in range(LEVELS):
        distance = 2**section
        far_keys, far_values = from_behind((key_local, value_local), "seq", distance)
        partner_ids = (device - distance) * blocks + jnp.arange(blocks, dtype=jnp.int32)
        carried = dense_set(carried, far_keys, far_values, partner_ids, False)
    running_max, running_sum, weighted = carried
    result = weighted / jnp.transpose(running_sum, (0, 2, 1))[..., None]
    result = result.astype(jnp.bfloat16).reshape(local_rows, head_count, head_width)
    return lax.all_to_all(result, "head", split_axis=0, concat_axis=1, tiled=True)


def solution(mesh):
    return jax.shard_map(
        local,
        mesh=mesh,
        in_specs=(
            P(("seq", "head"), None, None),
            P(("seq", "head"), None, None),
            P(("seq", "head"), None, None),
            P("seq", None),
        ),
        out_specs=P(("seq", "head"), None, None),
        check_vma=False,
    )
```

profile of v0, /device:TPU:4, one launch (start us, length us, event | category | flops | bytes accessed | tf_op | source)
XLA Modules:
  0.0 330.5 jit_solution(6914553099251389992)
XLA Ops:
  0.0 3.0 copy.31
  3.0 4.5 %all-to-all-start = ((bf16[64,64,128]{2,0,1:T(8,128)(2,1)}), bf16[64,64,128]{2,0,1:T(8,128)(2,1)S(1)}, u32[]{:S(2)}, u32[]{:S(2)}) async-start(bf16[64,64,128]{2,0,1:T(8,128)(2,1)} %copy.31), calls=%async_computation | async-start | bytes 2097152 | tf_op jit(solution)/shard_map/all_to_all | solution.py:32
  9.9 12.6 %all-to-all-done = bf16[64,64,128]{2,0,1:T(8,128)(2,1)S(1)} async-done(((bf16[64,64,128]{2,0,1:T(8,128)(2,1)}), bf16[64,64,128]{2,0,1:T(8,128)(2,1)S(1)}, u32[]{:S(2)}, u32[]{:S(2)}) %all-to-all-start) | async-done | bytes 1048608 | tf_op jit(solution)/shard_map/all_to_all | solution.py:32
  22.5 3.5 %all-to-all-start.1 = ((bf16[64,64,128]{2,0,1:T(8,128)(2,1)}), bf16[64,64,128]{2,0,1:T(8,128)(2,1)S(1)}, u32[]{:S(2)}, u32[]{:S(2)}) async-start(bf16[64,64,128]{2,0,1:T(8,128)(2,1)} %copy.33), calls=%async_computation.1 | async-start | bytes 2097152 | tf_op jit(solution)/shard_map/all_to_all | solution.py:31
  26.1 2.9 copy.35
  29.4 3.1 collective-permute-start.8
  32.5 7.8 %all-to-all-done.1 = bf16[64,64,128]{2,0,1:T(8,128)(2,1)S(1)} async-done(((bf16[64,64,128]{2,0,1:T(8,128)(2,1)}), bf16[64,64,128]{2,0,1:T(8,128)(2,1)S(1)}, u32[]{:S(2)}, u32[]{:S(2)}) %all-to-all-start.1) | async-done | bytes 1048608 | tf_op jit(solution)/shard_map/all_to_all | solution.py:31
  40.3 4.2 %all-to-all-start.2 = ((bf16[64,64,128]{2,0,1:T(8,128)(2,1)}), bf16[64,64,128]{2,0,1:T(8,128)(2,1)}, u32[]{:S(2)}, u32[]{:S(2)}) async-start(bf16[64,64,128]{2,0,1:T(8,128)(2,1)} %copy.35), calls=%async_computation.2 | async-start | bytes 2097152 | tf_op jit(solution)/shard_map/all_to_all | solution.py:33
  44.7 9.1 %collective-permute-start.6 = (bf16[256,16,128]{2,0,1:T(8,128)(2,1)S(1)}, bf16[256,16,128]{2,0,1:T(8,128)(2,1)}, u32[]{:S(2)}, u32[]{:S(2)}) collective-permute-start(bf16[256,16,128]{2,0,1:T(8,128)(2,1)S(1)} %bitcast.383), channel_id=1, source_target_pairs={{0,32},{4,36},{8,40},{12,44},{16,48},{20,52},{24,56},{28,60},{32,6... | collective-permute-start | bytes 3145736 | tf_op jit(solution)/shard_map/ppermute | solution.py:14
  54.1 3.4 %collective-permute-start.4 = (bf16[256,16,128]{2,0,1:T(8,128)(2,1)S(1)}, bf16[256,16,128]{2,0,1:T(8,128)(2,1)}, u32[]{:S(2)}, u32[]{:S(2)}) collective-permute-start(bf16[256,16,128]{2,0,1:T(8,128)(2,1)S(1)} %bitcast.384), channel_id=1, source_target_pairs={{0,16},{4,20},{8,24},{12,28},{16,32},{20,36},{24,40},{28,44},{32,4... | collective-permute-start | bytes 3145736 | tf_op jit(solution)/shard_map/ppermute | solution.py:14
  57.5 2.9 collective-permute-start.2
  64.6 3.0 collective-permute-done.8
  71.0 31.0 %collective-permute-done.6 = bf16[256,16,128]{2,0,1:T(8,128)(2,1)} collective-permute-done((bf16[256,16,128]{2,0,1:T(8,128)(2,1)S(1)}, bf16[256,16,128]{2,0,1:T(8,128)(2,1)}, u32[]{:S(2)}, u32[]{:S(2)}) %collective-permute-start.6) | collective-permute-done | bytes 1048608 | tf_op jit(solution)/shard_map/ppermute | solution.py:14
  105.9 38.9 %collective-permute-done.4 = bf16[256,16,128]{2,0,1:T(8,128)(2,1)} collective-permute-done((bf16[256,16,128]{2,0,1:T(8,128)(2,1)S(1)}, bf16[256,16,128]{2,0,1:T(8,128)(2,1)}, u32[]{:S(2)}, u32[]{:S(2)}) %collective-permute-start.4) | collective-permute-done | bytes 1048608 | tf_op jit(solution)/shard_map/ppermute | solution.py:14
  148.8 18.5 %collective-permute-done.2 = bf16[256,16,128]{2,0,1:T(8,128)(2,1)} collective-permute-done((bf16[256,16,128]{2,0,1:T(8,128)(2,1)S(1)}, bf16[256,16,128]{2,0,1:T(8,128)(2,1)}, u32[]{:S(2)}, u32[]{:S(2)}) %collective-permute-start.2) | collective-permute-done | bytes 1048608 | tf_op jit(solution)/shard_map/ppermute | solution.py:14
  171.7 15.7 %collective-permute-done = bf16[256,16,128]{2,0,1:T(8,128)(2,1)} collective-permute-done((bf16[256,16,128]{2,0,1:T(8,128)(2,1)S(1)}, bf16[256,16,128]{2,0,1:T(8,128)(2,1)}, u32[]{:S(2)}, u32[]{:S(2)}) %collective-permute-start) | collective-permute-done | bytes 1048608 | tf_op jit(solution)/shard_map/ppermute | solution.py:14
  187.4 6.5 %collective-permute-start.7 = (bf16[256,16,128]{2,0,1:T(8,128)(2,1)S(1)}, bf16[256,16,128]{2,0,1:T(8,128)(2,1)S(1)}, u32[]{:S(2)}, u32[]{:S(2)}) collective-permute-start(bf16[256,16,128]{2,0,1:T(8,128)(2,1)S(1)} %bitcast.378), channel_id=1, source_target_pairs={{0,32},{4,36},{8,40},{12,44},{16,48},{20,52},{24,56},{28,60},{32,6... | collective-permute-start | bytes 3145736 | tf_op jit(solution)/shard_map/ppermute | solution.py:14
  196.0 3.3 collective-permute-start.9
  204.2 16.8 %collective-permute-done.1 = bf16[256,16,128]{2,0,1:T(8,128)(2,1)S(1)} collective-permute-done((bf16[256,16,128]{2,0,1:T(8,128)(2,1)S(1)}, bf16[256,16,128]{2,0,1:T(8,128)(2,1)S(1)}, u32[]{:S(2)}, u32[]{:S(2)}) %collective-permute-start.1) | collective-permute-done | bytes 1048608 | tf_op jit(solution)/shard_map/ppermute | solution.py:14
  229.2 29.1 %collective-permute-done.7 = bf16[256,16,128]{2,0,1:T(8,128)(2,1)S(1)} collective-permute-done((bf16[256,16,128]{2,0,1:T(8,128)(2,1)S(1)}, bf16[256,16,128]{2,0,1:T(8,128)(2,1)S(1)}, u32[]{:S(2)}, u32[]{:S(2)}) %collective-permute-start.7) | collective-permute-done | bytes 1048608 | tf_op jit(solution)/shard_map/ppermute | solution.py:14
  259.7 13.5 %collective-permute-done.9 = bf16[256,16,128]{2,0,1:T(8,128)(2,1)S(1)} collective-permute-done((bf16[256,16,128]{2,0,1:T(8,128)(2,1)S(1)}, bf16[256,16,128]{2,0,1:T(8,128)(2,1)S(1)}, u32[]{:S(2)}, u32[]{:S(2)}) %collective-permute-start.9) | collective-permute-done | bytes 1048608 | tf_op jit(solution)/shard_map/ppermute | solution.py:14
  275.6 27.2 %collective-permute-done.11 = bf16[256,16,128]{2,0,1:T(8,128)(2,1)S(1)} collective-permute-done((bf16[256,16,128]{2,0,1:T(8,128)(2,1)S(1)}, bf16[256,16,128]{2,0,1:T(8,128)(2,1)S(1)}, u32[]{:S(2)}, u32[]{:S(2)}) %collective-permute-start.11) | collective-permute-done | bytes 1048608 | tf_op jit(solution)/shard_map/ppermute | solution.py:14
  302.9 5.6 %fusion.36 = bf16[2,128,16,128]{3,1,0,2:T(8,128)(2,1)S(1)} fusion(f32[16,2,128,128]{3,2,1,0:T(8,128)S(1)} %fusion.23, f32[16,2,128,128]{3,2,1,0:T(8,128)S(1)} %fusion.25, f32[16,2,128,128]{3,2,1,0:T(8,128)S(1)} %fusion.27, f32[16,2,128,128]{3,2,1,0:T(8,128)S(1)} %fusion.29, f32[16,2,128,128]{3,2,1,0:T(8,128)S(1)} %fusion.31, ...), kind=kOutput, calls=%fused_computation.44 | convolution fusion | flops 280494080 | bytes 19022336 | tf_op jit(solution)/shard_map/bhqn,nhd->bqhd/dot_general | solution.py:67
  309.2 20.0 %all_to_all.69 = bf16[256,16,128]{2,1,0:T(8,128)(2,1)S(1)} all-to-all(bf16[256,16,128]{2,1,0:T(8,128)(2,1)S(1)} %copy.44), channel_id=1, replica_groups=mesh['seq'=64,'head'=4] {'head'}, dimensions={0} | all-to-all | bytes 2097152 | tf_op jit(solution)/shard_map/all_to_all | solution.py:84
  (73 shorter events, 43.9 us)
Async XLA Ops:
  0.0 7.5 %copy-start = (bf16[64,64,128]{2,1,0:T(8,128)(2,1)S(1)}, bf16[64,64,128]{2,1,0:T(8,128)(2,1)}, u32[]{:S(2)}) copy-start(bf16[64,64,128]{2,1,0:T(8,128)(2,1)} %param.4) | copy-start | bytes 3145732
  0.0 9.2 %copy-start.1 = (s32[2,12]{1,0:T(2,128)S(1)}, s32[2,12]{1,0:T(2,128)}, u32[]{:S(2)}) copy-start(s32[2,12]{1,0:T(2,128)} %param.7) | copy-start | bytes 292
  3.0 19.6 %all-to-all-start = ((bf16[64,64,128]{2,0,1:T(8,128)(2,1)}), bf16[64,64,128]{2,0,1:T(8,128)(2,1)S(1)}, u32[]{:S(2)}, u32[]{:S(2)}) async-start(bf16[64,64,128]{2,0,1:T(8,128)(2,1)} %copy.31), calls=%async_computation | async-start | bytes 2097152 | tf_op jit(solution)/shard_map/all_to_all | solution.py:32
  22.5 17.7 %all-to-all-start.1 = ((bf16[64,64,128]{2,0,1:T(8,128)(2,1)}), bf16[64,64,128]{2,0,1:T(8,128)(2,1)S(1)}, u32[]{:S(2)}, u32[]{:S(2)}) async-start(bf16[64,64,128]{2,0,1:T(8,128)(2,1)} %copy.33), calls=%async_computation.1 | async-start | bytes 2097152 | tf_op jit(solution)/shard_map/all_to_all | solution.py:31
  29.4 38.2 %collective-permute-start.8 = (bf16[256,16,128]{2,0,1:T(8,128)(2,1)S(1)}, bf16[256,16,128]{2,0,1:T(8,128)(2,1)}, u32[]{:S(2)}, u32[]{:S(2)}) collective-permute-start(bf16[256,16,128]{2,0,1:T(8,128)(2,1)S(1)} %bitcast.382), channel_id=1, source_target_pairs={{0,64},{4,68},{8,72},{12,76},{16,80},{20,84},{24,88},{28,92},{32,9... | collective-permute-start | bytes 3145736 | tf_op jit(solution)/shard_map/ppermute | solution.py:14
  40.3 22.2 %all-to-all-start.2 = ((bf16[64,64,128]{2,0,1:T(8,128)(2,1)}), bf16[64,64,128]{2,0,1:T(8,128)(2,1)}, u32[]{:S(2)}, u32[]{:S(2)}) async-start(bf16[64,64,128]{2,0,1:T(8,128)(2,1)} %copy.35), calls=%async_computation.2 | async-start | bytes 2097152 | tf_op jit(solution)/shard_map/all_to_all | solution.py:33
  44.7 57.3 %collective-permute-start.6 = (bf16[256,16,128]{2,0,1:T(8,128)(2,1)S(1)}, bf16[256,16,128]{2,0,1:T(8,128)(2,1)}, u32[]{:S(2)}, u32[]{:S(2)}) collective-permute-start(bf16[256,16,128]{2,0,1:T(8,128)(2,1)S(1)} %bitcast.383), channel_id=1, source_target_pairs={{0,32},{4,36},{8,40},{12,44},{16,48},{20,52},{24,56},{28,60},{32,6... | collective-permute-start | bytes 3145736 | tf_op jit(solution)/shard_map/ppermute | solution.py:14
  54.1 90.7 %collective-permute-start.4 = (bf16[256,16,128]{2,0,1:T(8,128)(2,1)S(1)}, bf16[256,16,128]{2,0,1:T(8,128)(2,1)}, u32[]{:S(2)}, u32[]{:S(2)}) collective-permute-start(bf16[256,16,128]{2,0,1:T(8,128)(2,1)S(1)} %bitcast.384), channel_id=1, source_target_pairs={{0,16},{4,20},{8,24},{12,28},{16,32},{20,36},{24,40},{28,44},{32,4... | collective-permute-start | bytes 3145736 | tf_op jit(solution)/shard_map/ppermute | solution.py:14
  57.5 109.8 %collective-permute-start.2 = (bf16[256,16,128]{2,0,1:T(8,128)(2,1)S(1)}, bf16[256,16,128]{2,0,1:T(8,128)(2,1)}, u32[]{:S(2)}, u32[]{:S(2)}) collective-permute-start(bf16[256,16,128]{2,0,1:T(8,128)(2,1)S(1)} %bitcast.385), channel_id=1, source_target_pairs={{0,8},{4,12},{8,16},{12,20},{16,24},{20,28},{24,32},{28,36},{32,40... | collective-permute-start | bytes 3145736 | tf_op jit(solution)/shard_map/ppermute | solution.py:14
  60.5 127.0 %collective-permute-start = (bf16[256,16,128]{2,0,1:T(8,128)(2,1)S(1)}, bf16[256,16,128]{2,0,1:T(8,128)(2,1)}, u32[]{:S(2)}, u32[]{:S(2)}) collective-permute-start(bf16[256,16,128]{2,0,1:T(8,128)(2,1)S(1)} %bitcast.386), channel_id=1, source_target_pairs={{0,4},{4,8},{8,12},{12,16},{16,20},{20,24},{24,28},{28,32},{32,36}... | collective-permute-start | bytes 3145736 | tf_op jit(solution)/shard_map/ppermute | solution.py:14
  67.6 128.3 %collective-permute-start.10 = (bf16[256,16,128]{2,0,1:T(8,128)(2,1)S(1)}, bf16[256,16,128]{2,0,1:T(8,128)(2,1)S(1)}, u32[]{:S(2)}, u32[]{:S(2)}) collective-permute-start(bf16[256,16,128]{2,0,1:T(8,128)(2,1)S(1)} %bitcast.388), channel_id=1, source_target_pairs={{0,128},{4,132},{8,136},{12,140},{16,144},{20,148},{24,152},{28,15... | collective-permute-start | bytes 3145736 | tf_op jit(solution)/shard_map/ppermute | solution.py:14
  101.9 119.0 %collective-permute-start.1 = (bf16[256,16,128]{2,0,1:T(8,128)(2,1)S(1)}, bf16[256,16,128]{2,0,1:T(8,128)(2,1)S(1)}, u32[]{:S(2)}, u32[]{:S(2)}) collective-permute-start(bf16[256,16,128]{2,0,1:T(8,128)(2,1)S(1)} %bitcast.375), channel_id=1, source_target_pairs={{0,4},{4,8},{8,12},{12,16},{16,20},{20,24},{24,28},{28,32},{32,36}... | collective-permute-start | bytes 3145736 | tf_op jit(solution)/shard_map/ppermute | solution.py:14
  144.8 79.7 %collective-permute-start.3 = (bf16[256,16,128]{2,0,1:T(8,128)(2,1)S(1)}, bf16[256,16,128]{2,0,1:T(8,128)(2,1)S(1)}, u32[]{:S(2)}, u32[]{:S(2)}) collective-permute-start(bf16[256,16,128]{2,0,1:T(8,128)(2,1)S(1)} %bitcast.376), channel_id=1, source_target_pairs={{0,8},{4,12},{8,16},{12,20},{16,24},{20,28},{24,32},{28,36},{32,40... | collective-permute-start | bytes 3145736 | tf_op jit(solution)/shard_map/ppermute | solution.py:14
  167.3 59.6 %collective-permute-start.5 = (bf16[256,16,128]{2,0,1:T(8,128)(2,1)S(1)}, bf16[256,16,128]{2,0,1:T(8,128)(2,1)S(1)}, u32[]{:S(2)}, u32[]{:S(2)}) collective-permute-start(bf16[256,16,128]{2,0,1:T(8,128)(2,1)S(1)} %bitcast.377), channel_id=1, source_target_pairs={{0,16},{4,20},{8,24},{12,28},{16,32},{20,36},{24,40},{28,44},{32,4... | collective-permute-start | bytes 3145736 | tf_op jit(solution)/shard_map/ppermute | solution.py:14
  187.4 70.8 %collective-permute-start.7 = (bf16[256,16,128]{2,0,1:T(8,128)(2,1)S(1)}, bf16[256,16,128]{2,0,1:T(8,128)(2,1)S(1)}, u32[]{:S(2)}, u32[]{:S(2)}) collective-permute-start(bf16[256,16,128]{2,0,1:T(8,128)(2,1)S(1)} %bitcast.378), channel_id=1, source_target_pairs={{0,32},{4,36},{8,40},{12,44},{16,48},{20,52},{24,56},{28,60},{32,6... | collective-permute-start | bytes 3145736 | tf_op jit(solution)/shard_map/ppermute | solution.py:14
  196.0 77.2 %collective-permute-start.9 = (bf16[256,16,128]{2,0,1:T(8,128)(2,1)S(1)}, bf16[256,16,128]{2,0,1:T(8,128)(2,1)S(1)}, u32[]{:S(2)}, u32[]{:S(2)}) collective-permute-start(bf16[256,16,128]{2,0,1:T(8,128)(2,1)S(1)} %bitcast.379), channel_id=1, source_target_pairs={{0,64},{4,68},{8,72},{12,76},{16,80},{20,84},{24,88},{28,92},{32,9... | collective-permute-start | bytes 3145736 | tf_op jit(solution)/shard_map/ppermute | solution.py:14
  221.0 81.9 %collective-permute-start.11 = (bf16[256,16,128]{2,0,1:T(8,128)(2,1)S(1)}, bf16[256,16,128]{2,0,1:T(8,128)(2,1)S(1)}, u32[]{:S(2)}, u32[]{:S(2)}) collective-permute-start(bf16[256,16,128]{2,0,1:T(8,128)(2,1)S(1)} %bitcast.380), channel_id=1, source_target_pairs={{0,128},{4,132},{8,136},{12,140},{16,144},{20,148},{24,152},{28,15... | collective-permute-start | bytes 3145736 | tf_op jit(solution)/shard_map/ppermute | solution.py:14
where the time goes:
time: 331 us
  waiting for transfers between devices  214 us (65%)
  starting transfers between devices  51.2 us (15%)
  matrix products  25 us (8%)
  blocking collectives  20 us (6%)
  local copies, waits for them, and re-layouts  11.7 us (4%)
  other arithmetic  8.07 us (2%)
    ppermute x12, waiting for transfers between devices, from_behind(): return lax.ppermute(value, axis, pairs)  194 us
    ppermute x12, starting transfers between devices, from_behind(): return lax.ppermute(value, axis, pairs)  39 us
    all_to_all x1, blocking collectives, local(): lax.all_to_all(result, 'head', split_axis=0, concat_axis=1, tiled=True)  20 us
    dot_general x7, matrix products, apply_values(): jnp.einsum('bhqn,nhd->bqhd', rounded, near_values, preferred_element_type...  13.2 us
    all_to_all x1, waiting for transfers between devices, local(): lax.all_to_all(key_vectors, 'head', split_axis=1, concat_axis=0, tiled=True)  12.6 us
    dot_general x7, matrix products, dense_set(): jnp.einsum('bqhd,nhd->bhqn', query_tiles, near_keys, preferred_element_ty...  11.7 us
    unnamed x23, local copies, waits for them, and re-layouts  8.21 us
    all_to_all x1, waiting for transfers between devices, local(): lax.all_to_all(queries, 'head', split_axis=1, concat_axis=0, tiled=True)  7.77 us
  transfers between devices with their start and end apart: 15, of which 11 were waited for; matrix products, arithmetic and copies ran while one was open for 10% of the time, Pallas kernels for 0%

commit v1 on v0

--- a/solution.py
+++ b/solution.py
@@ -29,7 +29,12 @@
 def local(queries, key_vectors, value_vectors, key_blocks):
     query_local, key_local, value_local = (
         lax.all_to_all(queries, "head", split_axis=1, concat_axis=0, tiled=True),
-        lax.all_to_all(key_vectors, "head", split_axis=1, concat_axis=0, tiled=True),
+        jnp.concatenate(
+            lax.all_to_all(
+                jnp.stack(jnp.split(key_vectors, lax.axis_size("head"), axis=1)), "head", 0, 0
+            ),
+            axis=0,
+        ),
         lax.all_to_all(value_vectors, "head", split_axis=1, concat_axis=0, tiled=True),
     )
     local_rows, head_count, head_width = query_local.shape

time: 331 us -> 321 us (0.970)
  waiting for transfers between devices: 214 us -> 198 us
  starting transfers between devices: 51.2 us -> 57.3 us
    ppermute x12, waiting for transfers between devices: 194 us -> 184 us  [from_behind(): return lax.ppermute(value, axis, pairs)]
    all_to_all x1, waiting for transfers between devices: 7.77 us -> 1.59 us  [local(): lax.all_to_all(queries, 'head', split_axis=1, concat_axis=0, tiled=True)]
    ppermute x12, starting transfers between devices: 39 us -> 45.1 us  [from_behind(): return lax.ppermute(value, axis, pairs)]
    unnamed x23 -> x22, local copies, waits for them, and re-layouts: 8.21 us -> 5.22 us
  transfers between devices with their start and end apart: 15 -> 15, of which waited for: 11 -> 10; matrix products, arithmetic and copies ran while one was open for 10% -> 11% of each run, Pallas kernels for 0% -> 0%
where the time goes in v1:
time: 321 us; the launch traced here: 319 us
  waiting for transfers between devices  198 us (62%)
  starting transfers between devices  57.3 us (18%)
  matrix products  25.2 us (8%)
  blocking collectives  18.3 us (6%)
  local copies, waits for them, and re-layouts  10.4 us (3%)
  other arithmetic  9.19 us (3%)
    ppermute x12, waiting for transfers between devices, from_behind(): return lax.ppermute(value, axis, pairs)  184 us
    ppermute x12, starting transfers between devices, from_behind(): return lax.ppermute(value, axis, pairs)  45.1 us
    all_to_all x1, blocking collectives, local(): lax.all_to_all(result, 'head', split_axis=0, concat_axis=1, tiled=True)  18.3 us
    dot_general x7, matrix products, apply_values(): jnp.einsum('bhqn,nhd->bqhd', rounded, near_values, preferred_element_type...  13.5 us
    all_to_all x1, waiting for transfers between devices, local(): lax.all_to_all(jnp.stack(jnp.split(key_vectors, lax.axis_size('head'), ax...  12.7 us
    dot_general x7, matrix products, dense_set(): jnp.einsum('bqhd,nhd->bhqn', query_tiles, near_keys, preferred_element_ty...  11.7 us
    reduce_sum x7, other arithmetic, absorb(): running_sum = running_sum * factor + jnp.sum(weights, axis=-1)  7.06 us
  transfers between devices with their start and end apart: 15, of which 10 were waited for; matrix products, arithmetic and copies ran while one was open for 11% of the time, Pallas kernels for 0%

profile of v1, /device:TPU:4, one launch (start us, length us, event | category | flops | bytes accessed | tf_op | source)
XLA Modules:
  0.0 319.0 jit_solution(9467925757572603514)
XLA Ops:
  2.6 4.5 %all-to-all-start = ((bf16[4,64,16,128]{3,2,1,0:T(8,128)(2,1)}), bf16[4,64,16,128]{3,2,1,0:T(8,128)(2,1)S(1)}, u32[]{:S(2)}, u32[]{:S(2)}) async-start(bf16[4,64,16,128]{3,2,1,0:T(8,128)(2,1)} %pad_maximum_fusion), calls=%async_computation | async-start | bytes 2097152 | tf_op jit(solution)/shard_map/all_to_all | solution.py:33
  9.5 12.7 %all-to-all-done = bf16[4,64,16,128]{3,2,1,0:T(8,128)(2,1)S(1)} async-done(((bf16[4,64,16,128]{3,2,1,0:T(8,128)(2,1)}), bf16[4,64,16,128]{3,2,1,0:T(8,128)(2,1)S(1)}, u32[]{:S(2)}, u32[]{:S(2)}) %all-to-all-start) | async-done | bytes 1048608 | tf_op jit(solution)/shard_map/all_to_all | solution.py:33
  22.2 3.5 %all-to-all-start.1 = ((bf16[64,64,128]{2,0,1:T(8,128)(2,1)}), bf16[64,64,128]{2,0,1:T(8,128)(2,1)S(1)}, u32[]{:S(2)}, u32[]{:S(2)}) async-start(bf16[64,64,128]{2,0,1:T(8,128)(2,1)} %copy.31), calls=%async_computation.1 | async-start | bytes 2097152 | tf_op jit(solution)/shard_map/all_to_all | solution.py:31
  25.8 2.9 copy.33
  29.2 9.1 %collective-permute-start.6 = (bf16[256,16,128]{2,0,1:T(8,128)(2,1)S(1)}, bf16[256,16,128]{2,0,1:T(8,128)(2,1)}, u32[]{:S(2)}, u32[]{:S(2)}) collective-permute-start(bf16[256,16,128]{2,0,1:T(8,128)(2,1)S(1)} %bitcast.387), channel_id=1, source_target_pairs={{0,32},{4,36},{8,40},{12,44},{16,48},{20,52},{24,56},{28,60},{32,6... | collective-permute-start | bytes 3145736 | tf_op jit(solution)/shard_map/ppermute | solution.py:14
  39.9 4.2 %all-to-all-start.2 = ((bf16[64,64,128]{2,0,1:T(8,128)(2,1)}), bf16[64,64,128]{2,0,1:T(8,128)(2,1)}, u32[]{:S(2)}, u32[]{:S(2)}) async-start(bf16[64,64,128]{2,0,1:T(8,128)(2,1)} %copy.33), calls=%async_computation.2 | async-start | bytes 2097152 | tf_op jit(solution)/shard_map/all_to_all | solution.py:38
  44.3 5.2 %collective-permute-start.4 = (bf16[256,16,128]{2,0,1:T(8,128)(2,1)S(1)}, bf16[256,16,128]{2,0,1:T(8,128)(2,1)}, u32[]{:S(2)}, u32[]{:S(2)}) collective-permute-start(bf16[256,16,128]{2,0,1:T(8,128)(2,1)S(1)} %bitcast.388), channel_id=1, source_target_pairs={{0,16},{4,20},{8,24},{12,28},{16,32},{20,36},{24,40},{28,44},{32,4... | collective-permute-start | bytes 3145736 | tf_op jit(solution)/shard_map/ppermute | solution.py:14
  49.8 3.8 %collective-permute-start.2 = (bf16[256,16,128]{2,0,1:T(8,128)(2,1)S(1)}, bf16[256,16,128]{2,0,1:T(8,128)(2,1)}, u32[]{:S(2)}, u32[]{:S(2)}) collective-permute-start(bf16[256,16,128]{2,0,1:T(8,128)(2,1)S(1)} %bitcast.389), channel_id=1, source_target_pairs={{0,8},{4,12},{8,16},{12,20},{16,24},{20,28},{24,32},{28,36},{32,40... | collective-permute-start | bytes 3145736 | tf_op jit(solution)/shard_map/ppermute | solution.py:14
  55.6 3.1 collective-permute-start.8
  60.9 23.5 %collective-permute-done.6 = bf16[256,16,128]{2,0,1:T(8,128)(2,1)} collective-permute-done((bf16[256,16,128]{2,0,1:T(8,128)(2,1)S(1)}, bf16[256,16,128]{2,0,1:T(8,128)(2,1)}, u32[]{:S(2)}, u32[]{:S(2)}) %collective-permute-start.6) | collective-permute-done | bytes 1048608 | tf_op jit(solution)/shard_map/ppermute | solution.py:14
  87.7 41.6 %collective-permute-done.4 = bf16[256,16,128]{2,0,1:T(8,128)(2,1)} collective-permute-done((bf16[256,16,128]{2,0,1:T(8,128)(2,1)S(1)}, bf16[256,16,128]{2,0,1:T(8,128)(2,1)}, u32[]{:S(2)}, u32[]{:S(2)}) %collective-permute-start.4) | collective-permute-done | bytes 1048608 | tf_op jit(solution)/shard_map/ppermute | solution.py:14
  133.3 18.5 %collective-permute-done.2 = bf16[256,16,128]{2,0,1:T(8,128)(2,1)} collective-permute-done((bf16[256,16,128]{2,0,1:T(8,128)(2,1)S(1)}, bf16[256,16,128]{2,0,1:T(8,128)(2,1)}, u32[]{:S(2)}, u32[]{:S(2)}) %collective-permute-start.2) | collective-permute-done | bytes 1048608 | tf_op jit(solution)/shard_map/ppermute | solution.py:14
  151.8 4.5 %collective-permute-start.3 = (bf16[256,16,128]{2,0,1:T(8,128)(2,1)S(1)}, bf16[256,16,128]{2,0,1:T(8,128)(2,1)S(1)}, u32[]{:S(2)}, u32[]{:S(2)}) collective-permute-start(bf16[256,16,128]{2,0,1:T(8,128)(2,1)S(1)} %bitcast.381), channel_id=1, source_target_pairs={{0,8},{4,12},{8,16},{12,20},{16,24},{20,28},{24,32},{28,36},{32,40... | collective-permute-start | bytes 3145736 | tf_op jit(solution)/shard_map/ppermute | solution.py:14
  158.3 5.4 %collective-permute-done = bf16[256,16,128]{2,0,1:T(8,128)(2,1)} collective-permute-done((bf16[256,16,128]{2,0,1:T(8,128)(2,1)S(1)}, bf16[256,16,128]{2,0,1:T(8,128)(2,1)}, u32[]{:S(2)}, u32[]{:S(2)}) %collective-permute-start) | collective-permute-done | bytes 1048608 | tf_op jit(solution)/shard_map/ppermute | solution.py:14
  163.7 7.3 %collective-permute-start.5 = (bf16[256,16,128]{2,0,1:T(8,128)(2,1)S(1)}, bf16[256,16,128]{2,0,1:T(8,128)(2,1)S(1)}, u32[]{:S(2)}, u32[]{:S(2)}) collective-permute-start(bf16[256,16,128]{2,0,1:T(8,128)(2,1)S(1)} %bitcast.382), channel_id=1, source_target_pairs={{0,16},{4,20},{8,24},{12,28},{16,32},{20,36},{24,40},{28,44},{32,4... | collective-permute-start | bytes 3145736 | tf_op jit(solution)/shard_map/ppermute | solution.py:14
  173.1 3.6 %collective-permute-start.7 = (bf16[256,16,128]{2,0,1:T(8,128)(2,1)S(1)}, bf16[256,16,128]{2,0,1:T(8,128)(2,1)S(1)}, u32[]{:S(2)}, u32[]{:S(2)}) collective-permute-start(bf16[256,16,128]{2,0,1:T(8,128)(2,1)S(1)} %bitcast.383), channel_id=1, source_target_pairs={{0,32},{4,36},{8,40},{12,44},{16,48},{20,52},{24,56},{28,60},{32,6... | collective-permute-start | bytes 3145736 | tf_op jit(solution)/shard_map/ppermute | solution.py:14
  176.6 2.0 fusion.19
  178.7 16.8 %collective-permute-done.10 = bf16[256,16,128]{2,0,1:T(8,128)(2,1)S(1)} collective-permute-done((bf16[256,16,128]{2,0,1:T(8,128)(2,1)S(1)}, bf16[256,16,128]{2,0,1:T(8,128)(2,1)S(1)}, u32[]{:S(2)}, u32[]{:S(2)}) %collective-permute-start.10) | collective-permute-done | bytes 1048608 | tf_op jit(solution)/shard_map/ppermute | solution.py:14
  195.5 2.1 collective-permute-start.9
  208.5 5.5 %collective-permute-done.5 = bf16[256,16,128]{2,0,1:T(8,128)(2,1)S(1)} collective-permute-done((bf16[256,16,128]{2,0,1:T(8,128)(2,1)S(1)}, bf16[256,16,128]{2,0,1:T(8,128)(2,1)S(1)}, u32[]{:S(2)}, u32[]{:S(2)}) %collective-permute-start.5) | collective-permute-done | bytes 1048608 | tf_op jit(solution)/shard_map/ppermute | solution.py:14
  216.3 32.1 %collective-permute-done.7 = bf16[256,16,128]{2,0,1:T(8,128)(2,1)S(1)} collective-permute-done((bf16[256,16,128]{2,0,1:T(8,128)(2,1)S(1)}, bf16[256,16,128]{2,0,1:T(8,128)(2,1)S(1)}, u32[]{:S(2)}, u32[]{:S(2)}) %collective-permute-start.7) | collective-permute-done | bytes 1048608 | tf_op jit(solution)/shard_map/ppermute | solution.py:14
  249.8 40.5 %collective-permute-done.9 = bf16[256,16,128]{2,0,1:T(8,128)(2,1)S(1)} collective-permute-done((bf16[256,16,128]{2,0,1:T(8,128)(2,1)S(1)}, bf16[256,16,128]{2,0,1:T(8,128)(2,1)S(1)}, u32[]{:S(2)}, u32[]{:S(2)}) %collective-permute-start.9) | collective-permute-done | bytes 1048608 | tf_op jit(solution)/shard_map/ppermute | solution.py:14
  292.8 5.9 %fusion.36 = bf16[2,128,16,128]{3,1,0,2:T(8,128)(2,1)S(1)} fusion(f32[16,2,128,128]{3,2,1,0:T(8,128)S(1)} %fusion.23, f32[16,2,128,128]{3,2,1,0:T(8,128)S(1)} %fusion.25, f32[16,2,128,128]{3,2,1,0:T(8,128)S(1)} %fusion.27, f32[16,2,128,128]{3,2,1,0:T(8,128)S(1)} %fusion.29, f32[16,2,128,128]{3,2,1,0:T(8,128)S(1)} %fusion.31, ...), kind=kOutput, calls=%fused_computation.44 | convolution fusion | flops 280494080 | bytes 19022336 | tf_op jit(solution)/shard_map/bhqn,nhd->bqhd/dot_general | solution.py:72
  299.4 18.3 %all_to_all.56 = bf16[256,16,128]{2,1,0:T(8,128)(2,1)S(1)} all-to-all(bf16[256,16,128]{2,1,0:T(8,128)(2,1)S(1)} %copy.42), channel_id=1, replica_groups=mesh['seq'=64,'head'=4] {'head'}, dimensions={0} | all-to-all | bytes 2097152 | tf_op jit(solution)/shard_map/all_to_all | solution.py:89
  (74 shorter events, 41.9 us)
Async XLA Ops:
  0.0 7.2 %copy-start = (bf16[64,64,128]{2,1,0:T(8,128)(2,1)S(1)}, bf16[64,64,128]{2,1,0:T(8,128)(2,1)}, u32[]{:S(2)}) copy-start(bf16[64,64,128]{2,1,0:T(8,128)(2,1)} %param.4) | copy-start | bytes 3145732
  0.0 8.8 %copy-start.1 = (s32[2,12]{1,0:T(2,128)S(1)}, s32[2,12]{1,0:T(2,128)}, u32[]{:S(2)}) copy-start(s32[2,12]{1,0:T(2,128)} %param.7) | copy-start | bytes 292
  2.6 19.6 %all-to-all-start = ((bf16[4,64,16,128]{3,2,1,0:T(8,128)(2,1)}), bf16[4,64,16,128]{3,2,1,0:T(8,128)(2,1)S(1)}, u32[]{:S(2)}, u32[]{:S(2)}) async-start(bf16[4,64,16,128]{3,2,1,0:T(8,128)(2,1)} %pad_maximum_fusion), calls=%async_computation | async-start | bytes 2097152 | tf_op jit(solution)/shard_map/all_to_all | solution.py:33
  22.2 17.7 %all-to-all-start.1 = ((bf16[64,64,128]{2,0,1:T(8,128)(2,1)}), bf16[64,64,128]{2,0,1:T(8,128)(2,1)S(1)}, u32[]{:S(2)}, u32[]{:S(2)}) async-start(bf16[64,64,128]{2,0,1:T(8,128)(2,1)} %copy.31), calls=%async_computation.1 | async-start | bytes 2097152 | tf_op jit(solution)/shard_map/all_to_all | solution.py:31
  29.2 55.2 %collective-permute-start.6 = (bf16[256,16,128]{2,0,1:T(8,128)(2,1)S(1)}, bf16[256,16,128]{2,0,1:T(8,128)(2,1)}, u32[]{:S(2)}, u32[]{:S(2)}) collective-permute-start(bf16[256,16,128]{2,0,1:T(8,128)(2,1)S(1)} %bitcast.387), channel_id=1, source_target_pairs={{0,32},{4,36},{8,40},{12,44},{16,48},{20,52},{24,56},{28,60},{32,6... | collective-permute-start | bytes 3145736 | tf_op jit(solution)/shard_map/ppermute | solution.py:14
  39.9 18.9 %all-to-all-start.2 = ((bf16[64,64,128]{2,0,1:T(8,128)(2,1)}), bf16[64,64,128]{2,0,1:T(8,128)(2,1)}, u32[]{:S(2)}, u32[]{:S(2)}) async-start(bf16[64,64,128]{2,0,1:T(8,128)(2,1)} %copy.33), calls=%async_computation.2 | async-start | bytes 2097152 | tf_op jit(solution)/shard_map/all_to_all | solution.py:38
  44.3 85.0 %collective-permute-start.4 = (bf16[256,16,128]{2,0,1:T(8,128)(2,1)S(1)}, bf16[256,16,128]{2,0,1:T(8,128)(2,1)}, u32[]{:S(2)}, u32[]{:S(2)}) collective-permute-start(bf16[256,16,128]{2,0,1:T(8,128)(2,1)S(1)} %bitcast.388), channel_id=1, source_target_pairs={{0,16},{4,20},{8,24},{12,28},{16,32},{20,36},{24,40},{28,44},{32,4... | collective-permute-start | bytes 3145736 | tf_op jit(solution)/shard_map/ppermute | solution.py:14
  49.8 101.9 %collective-permute-start.2 = (bf16[256,16,128]{2,0,1:T(8,128)(2,1)S(1)}, bf16[256,16,128]{2,0,1:T(8,128)(2,1)}, u32[]{:S(2)}, u32[]{:S(2)}) collective-permute-start(bf16[256,16,128]{2,0,1:T(8,128)(2,1)S(1)} %bitcast.389), channel_id=1, source_target_pairs={{0,8},{4,12},{8,16},{12,20},{16,24},{20,28},{24,32},{28,36},{32,40... | collective-permute-start | bytes 3145736 | tf_op jit(solution)/shard_map/ppermute | solution.py:14
  53.7 110.0 %collective-permute-start = (bf16[256,16,128]{2,0,1:T(8,128)(2,1)S(1)}, bf16[256,16,128]{2,0,1:T(8,128)(2,1)}, u32[]{:S(2)}, u32[]{:S(2)}) collective-permute-start(bf16[256,16,128]{2,0,1:T(8,128)(2,1)S(1)} %bitcast.390), channel_id=1, source_target_pairs={{0,4},{4,8},{8,12},{12,16},{16,20},{20,24},{24,28},{28,32},{32,36}... | collective-permute-start | bytes 3145736 | tf_op jit(solution)/shard_map/ppermute | solution.py:14
  55.6 117.4 %collective-permute-start.8 = (bf16[256,16,128]{2,0,1:T(8,128)(2,1)S(1)}, bf16[256,16,128]{2,0,1:T(8,128)(2,1)}, u32[]{:S(2)}, u32[]{:S(2)}) collective-permute-start(bf16[256,16,128]{2,0,1:T(8,128)(2,1)S(1)} %bitcast.391), channel_id=1, source_target_pairs={{0,64},{4,68},{8,72},{12,76},{16,80},{20,84},{24,88},{28,92},{32,9... | collective-permute-start | bytes 3145736 | tf_op jit(solution)/shard_map/ppermute | solution.py:14
  84.4 111.1 %collective-permute-start.10 = (bf16[256,16,128]{2,0,1:T(8,128)(2,1)S(1)}, bf16[256,16,128]{2,0,1:T(8,128)(2,1)S(1)}, u32[]{:S(2)}, u32[]{:S(2)}) collective-permute-start(bf16[256,16,128]{2,0,1:T(8,128)(2,1)S(1)} %bitcast.393), channel_id=1, source_target_pairs={{0,128},{4,132},{8,136},{12,140},{16,144},{20,148},{24,152},{28,15... | collective-permute-start | bytes 3145736 | tf_op jit(solution)/shard_map/ppermute | solution.py:14
  129.3 73.3 %collective-permute-start.1 = (bf16[256,16,128]{2,0,1:T(8,128)(2,1)S(1)}, bf16[256,16,128]{2,0,1:T(8,128)(2,1)S(1)}, u32[]{:S(2)}, u32[]{:S(2)}) collective-permute-start(bf16[256,16,128]{2,0,1:T(8,128)(2,1)S(1)} %bitcast.380), channel_id=1, source_target_pairs={{0,4},{4,8},{8,12},{12,16},{16,20},{20,24},{24,28},{28,32},{32,36}... | collective-permute-start | bytes 3145736 | tf_op jit(solution)/shard_map/ppermute | solution.py:14
  151.8 54.4 %collective-permute-start.3 = (bf16[256,16,128]{2,0,1:T(8,128)(2,1)S(1)}, bf16[256,16,128]{2,0,1:T(8,128)(2,1)S(1)}, u32[]{:S(2)}, u32[]{:S(2)}) collective-permute-start(bf16[256,16,128]{2,0,1:T(8,128)(2,1)S(1)} %bitcast.381), channel_id=1, source_target_pairs={{0,8},{4,12},{8,16},{12,20},{16,24},{20,28},{24,32},{28,36},{32,40... | collective-permute-start | bytes 3145736 | tf_op jit(solution)/shard_map/ppermute | solution.py:14
  163.7 50.3 %collective-permute-start.5 = (bf16[256,16,128]{2,0,1:T(8,128)(2,1)S(1)}, bf16[256,16,128]{2,0,1:T(8,128)(2,1)S(1)}, u32[]{:S(2)}, u32[]{:S(2)}) collective-permute-start(bf16[256,16,128]{2,0,1:T(8,128)(2,1)S(1)} %bitcast.382), channel_id=1, source_target_pairs={{0,16},{4,20},{8,24},{12,28},{16,32},{20,36},{24,40},{28,44},{32,4... | collective-permute-start | bytes 3145736 | tf_op jit(solution)/shard_map/ppermute | solution.py:14
  173.1 75.4 %collective-permute-start.7 = (bf16[256,16,128]{2,0,1:T(8,128)(2,1)S(1)}, bf16[256,16,128]{2,0,1:T(8,128)(2,1)S(1)}, u32[]{:S(2)}, u32[]{:S(2)}) collective-permute-start(bf16[256,16,128]{2,0,1:T(8,128)(2,1)S(1)} %bitcast.383), channel_id=1, source_target_pairs={{0,32},{4,36},{8,40},{12,44},{16,48},{20,52},{24,56},{28,60},{32,6... | collective-permute-start | bytes 3145736 | tf_op jit(solution)/shard_map/ppermute | solution.py:14
  195.5 94.8 %collective-permute-start.9 = (bf16[256,16,128]{2,0,1:T(8,128)(2,1)S(1)}, bf16[256,16,128]{2,0,1:T(8,128)(2,1)S(1)}, u32[]{:S(2)}, u32[]{:S(2)}) collective-permute-start(bf16[256,16,128]{2,0,1:T(8,128)(2,1)S(1)} %bitcast.384), channel_id=1, source_target_pairs={{0,64},{4,68},{8,72},{12,76},{16,80},{20,84},{24,88},{28,92},{32,9... | collective-permute-start | bytes 3145736 | tf_op jit(solution)/shard_map/ppermute | solution.py:14
  202.6 90.3 %collective-permute-start.11 = (bf16[256,16,128]{2,0,1:T(8,128)(2,1)S(1)}, bf16[256,16,128]{2,0,1:T(8,128)(2,1)S(1)}, u32[]{:S(2)}, u32[]{:S(2)}) collective-permute-start(bf16[256,16,128]{2,0,1:T(8,128)(2,1)S(1)} %bitcast.385), channel_id=1, source_target_pairs={{0,128},{4,132},{8,136},{12,140},{16,144},{20,148},{24,152},{28,15... | collective-permute-start | bytes 3145736 | tf_op jit(solution)/shard_map/ppermute | solution.py:14
